TPU v7x, 256 devices: a whole 4x4x8 slice. The times are simulated.
256 devices in a mesh: row: 8 (over x, core), col: 32 (over y, z).
Axes of the slice: x: 4, y: 4, z: 8, core: 2. Of those that a mesh axis runs over, the one named last changes fastest.
Arguments:
- upper_panel: float32 [2048, 8192], P('row', 'col')
- lower_panel: float32 [2048, 8192], P('row', 'col')
- pole_values: float32 [2, 8192], P(None, 'col'), may hold values from 0 to 4, as said below
- coupling: float32 [2, 8192], P(None, 'col'), may hold values from -6 to 6
- kept_mask: int32 [2, 8192], P(None, 'col'), may hold values from 0 to 1, as said below
- shifts: float32 [16384], P('col'), may hold values from 0 to 4
- source: int32 [16384], P('col'), may hold values from 0 to 16384, as said below
Outputs:
- vectors: float32 [2, 2048, 16384], P(None, 'row', 'col')
- slab_weight: float32 [16384], P('col')
Inputs may be any that keep to these rules, and one draw needn't show every extreme that they name: source[j] = 16384 marks an undeflated merged column; any other value is the pole whose child column the merged column copies, and no pole is named twice. Each device's 512 merged columns hold from 64 to 384 undeflated columns, and some device holds exactly 384. kept_mask is 0 exactly at the poles named in source. Some device of col holds no deflated pole: every pole of both children that it holds is kept. `pole_values`: every pole lies at least 0.4 / 16384 away from every entry of shifts.
All inputs are finite; a program needn't handle non-finite values.
Results may differ from a plain program's by a relative error of at most 0.0003.
Values sent between devices are 32-bit elements; how exact they have to be, the bound alone decides.
A program may use at most 64 MiB of HBM per device.

v0:
```python
import math

import jax
import jax.numpy as jnp
from jax import lax
from jax.sharding import PartitionSpec as P

N1 = 8192


exact_mode = lax.Precision.HIGHEST


def cauchy_block(pole_vals, weights, shift_vals):
    return weights[:, :, None] / (pole_vals[:, :, None] - shift_vals[None, None, :])


def local(upper_panel, lower_panel, pole_values, coupling, kept_mask, shifts, source):
    rows_here = upper_panel.shape[0]
    own_cols = shifts.shape[0]
    weighted = coupling * kept_mask.astype(jnp.float32)
    undeflated = source == 2 * N1
    child_base = jnp.array([0, N1], jnp.int32)
    zeros_acc = jnp.zeros((rows_here, own_cols), jnp.float32)
    pieces = (
        lax.all_gather(upper_panel, "col", axis=1, tiled=True),
        lax.all_gather(lower_panel, "col", axis=1, tiled=True),
        lax.all_gather(pole_values, "col", axis=1, tiled=True),
        lax.all_gather(weighted, "col", axis=1, tiled=True),
    )
    span_cols = math.gcd(pieces[0].shape[1], 1024)

    def advance(number, running):
        window = [
            lax.dynamic_slice_in_dim(member, number * span_cols, span_cols, 1) for member in pieces
        ]
        first_pole = number * span_cols
        cauchy = cauchy_block(window[2], window[3], shifts)
        indices = first_pole + lax.iota(jnp.int32, span_cols)
        one_hot = indices[None, :, None] + child_base[:, None, None] == source[None, None, :]
        basis_tile = jnp.where(undeflated[None, None, :], cauchy, one_hot.astype(jnp.float32))
        upper_acc = running[0] + jnp.dot(
            window[0], basis_tile[0], precision=exact_mode, preferred_element_type=jnp.float32
        )
        lower_acc = running[1] + jnp.dot(
            window[1], basis_tile[1], precision=exact_mode, preferred_element_type=jnp.float32
        )
        return (upper_acc, lower_acc, running[2] + jnp.sum(cauchy * cauchy, axis=(0, 1)))

    upper_acc, lower_acc, norm_sums = lax.fori_loop(
        0,
        pieces[0].shape[1] // span_cols,
        advance,
        (zeros_acc, zeros_acc, jnp.zeros((own_cols,), jnp.float32)),
    )
    scaling = jnp.where(undeflated, lax.rsqrt(norm_sums), 1.0)
    vectors = jnp.stack([upper_acc * scaling[None, :], lower_acc * scaling[None, :]])
    partial_weight = jnp.sum(vectors * vectors, axis=(0, 1))
    slab_weight = lax.psum(partial_weight, "row") / (2 * rows_here * lax.axis_size("row"))
    return (vectors, slab_weight)


def solution(mesh):
    in_specs = (
        P("row", "col"),
        P("row", "col"),
        P(None, "col"),
        P(None, "col"),
        P(None, "col"),
        P("col"),
        P("col"),
    )
    out_specs = (P(None, "row", "col"), P("col"))
    return jax.shard_map(local, mesh=mesh, in_specs=in_specs, out_specs=out_specs, check_vma=False)
```

profile of v0, /device:TPU:1, one launch (start us, length us, event | category | flops | bytes accessed | tf_op | source)
XLA Modules:
  0.0 310.2 jit_solution(16482954497444541827)
XLA Ops:
  9.4 41.5 %all_gather.13 = f32[2,8192]{1,0:T(2,128)S(1)} all-gather(f32[2,256]{1,0:T(2,128)S(1)} %convert_multiply_fusion), channel_id=1, replica_groups=mesh['row'=8,'col'=32] {'col'}, dimensions={1}, use_global_device_ids=true | all-gather | bytes 67584 | tf_op jit(solution)/shard_map/all_gather | solution.py:29
  50.9 39.2 %all_gather.14 = f32[2,8192]{1,0:T(2,128)S(1)} all-gather(f32[2,256]{1,0:T(2,128)} %param.12), channel_id=1, replica_groups=mesh['row'=8,'col'=32] {'col'}, dimensions={1}, use_global_device_ids=true | all-gather | bytes 67584 | tf_op jit(solution)/shard_map/all_gather | solution.py:28
  90.8 23.1 %all-gather.3.cloned.1.call-done = f32[256,8192]{1,0:T(8,128)} async-done(((f32[256,256]{1,0:T(8,128)}), f32[256,8192]{1,0:T(8,128)}) %all-gather.3.cloned.1.call-update) | async-done | bytes 8388624 | tf_op jit(solution)/shard_map/all_gather | solution.py:26
  113.9 102.9 %all-gather.5.cloned.1.call-done = f32[256,8192]{1,0:T(8,128)} async-done(((f32[256,256]{1,0:T(8,128)}), f32[256,8192]{1,0:T(8,128)}) %all-gather.5.cloned.1.call-update) | async-done | bytes 8388624 | tf_op jit(solution)/shard_map/all_gather | solution.py:27
  216.8 68.3 %while.18 = (s32[]{:T(128)}, f32[256,512]{1,0:T(8,128)S(1)}, f32[256,512]{1,0:T(8,128)S(1)}, f32[512]{0:T(512)S(1)}, f32[256,8192]{1,0:T(8,128)}, /*index=5*/pre...) while((s32[]{:T(128)}, f32[256,512]{1,0:T(8,128)S(1)}, ...), condition=%wide.region_2.3_spmd.clone, body=%wide.region_0.2_spmd.clone.sunk | while | flops 3229093376 | bytes 12669679 | solution.py:50
  218.8 3.3 %fusion.17 = f32[256,512]{1,0:T(8,128)S(1)} fusion(f32[2,1024,512]{2,1,0:T(8,128)S(1)} %get-tuple-element.347, f32[256,8192]{1,0:T(8,128)} %get-tuple-element.389, s32[]{:T(128)S(6)} %select_n.28, f32[256,512]{1,0:T(8,128)S(1)} %get-tuple-element.366, pred[]{:T(512)S(6)} %compare.3), kind=kOutput, calls=%fused_computation.9.clone.1 | convolution fusion | flops 1610874880 | bytes 4194309 | tf_op jit(solution)/shard_map/while/body/eval_jaxpr/dot_general | solution.py:45
  222.1 3.3 %fusion.16 = f32[256,512]{1,0:T(8,128)S(1)} fusion(f32[2,1024,512]{2,1,0:T(8,128)S(1)} %get-tuple-element.347, f32[256,8192]{1,0:T(8,128)} %get-tuple-element.383, s32[]{:T(128)S(6)} %select_n.28, f32[256,512]{1,0:T(8,128)S(1)} %get-tuple-element.365, pred[]{:T(512)S(6)} %compare.3), kind=kOutput, calls=%fused_computation.8.clone.1 | convolution fusion | flops 1610874880 | bytes 4194309 | tf_op jit(solution)/shard_map/while/body/eval_jaxpr/dot_general | solution.py:42
  225.5 1.9 multiply_reduce_fusion.3
  227.4 3.3 %fusion.17 = f32[256,512]{1,0:T(8,128)S(1)} fusion(f32[2,1024,512]{2,1,0:T(8,128)S(1)} %get-tuple-element.347, f32[256,8192]{1,0:T(8,128)} %get-tuple-element.389, s32[]{:T(128)S(6)} %select_n.28, f32[256,512]{1,0:T(8,128)S(1)} %get-tuple-element.366, pred[]{:T(512)S(6)} %compare.3), kind=kOutput, calls=%fused_computation.9.clone.1 | convolution fusion | flops 1610874880 | bytes 4194309 | tf_op jit(solution)/shard_map/while/body/eval_jaxpr/dot_general | solution.py:45
  230.6 3.3 %fusion.16 = f32[256,512]{1,0:T(8,128)S(1)} fusion(f32[2,1024,512]{2,1,0:T(8,128)S(1)} %get-tuple-element.347, f32[256,8192]{1,0:T(8,128)} %get-tuple-element.383, s32[]{:T(128)S(6)} %select_n.28, f32[256,512]{1,0:T(8,128)S(1)} %get-tuple-element.365, pred[]{:T(512)S(6)} %compare.3), kind=kOutput, calls=%fused_computation.8.clone.1 | convolution fusion | flops 1610874880 | bytes 4194309 | tf_op jit(solution)/shard_map/while/body/eval_jaxpr/dot_general | solution.py:42
  235.9 3.3 %fusion.17 = f32[256,512]{1,0:T(8,128)S(1)} fusion(f32[2,1024,512]{2,1,0:T(8,128)S(1)} %get-tuple-element.347, f32[256,8192]{1,0:T(8,128)} %get-tuple-element.389, s32[]{:T(128)S(6)} %select_n.28, f32[256,512]{1,0:T(8,128)S(1)} %get-tuple-element.366, pred[]{:T(512)S(6)} %compare.3), kind=kOutput, calls=%fused_computation.9.clone.1 | convolution fusion | flops 1610874880 | bytes 4194309 | tf_op jit(solution)/shard_map/while/body/eval_jaxpr/dot_general | solution.py:45
  239.2 3.3 %fusion.16 = f32[256,512]{1,0:T(8,128)S(1)} fusion(f32[2,1024,512]{2,1,0:T(8,128)S(1)} %get-tuple-element.347, f32[256,8192]{1,0:T(8,128)} %get-tuple-element.383, s32[]{:T(128)S(6)} %select_n.28, f32[256,512]{1,0:T(8,128)S(1)} %get-tuple-element.365, pred[]{:T(512)S(6)} %compare.3), kind=kOutput, calls=%fused_computation.8.clone.1 | convolution fusion | flops 1610874880 | bytes 4194309 | tf_op jit(solution)/shard_map/while/body/eval_jaxpr/dot_general | solution.py:42
  242.6 1.9 multiply_reduce_fusion.3
  244.5 3.3 %fusion.17 = f32[256,512]{1,0:T(8,128)S(1)} fusion(f32[2,1024,512]{2,1,0:T(8,128)S(1)} %get-tuple-element.347, f32[256,8192]{1,0:T(8,128)} %get-tuple-element.389, s32[]{:T(128)S(6)} %select_n.28, f32[256,512]{1,0:T(8,128)S(1)} %get-tuple-element.366, pred[]{:T(512)S(6)} %compare.3), kind=kOutput, calls=%fused_computation.9.clone.1 | convolution fusion | flops 1610874880 | bytes 4194309 | tf_op jit(solution)/shard_map/while/body/eval_jaxpr/dot_general | solution.py:45
  247.7 3.3 %fusion.16 = f32[256,512]{1,0:T(8,128)S(1)} fusion(f32[2,1024,512]{2,1,0:T(8,128)S(1)} %get-tuple-element.347, f32[256,8192]{1,0:T(8,128)} %get-tuple-element.383, s32[]{:T(128)S(6)} %select_n.28, f32[256,512]{1,0:T(8,128)S(1)} %get-tuple-element.365, pred[]{:T(512)S(6)} %compare.3), kind=kOutput, calls=%fused_computation.8.clone.1 | convolution fusion | flops 1610874880 | bytes 4194309 | tf_op jit(solution)/shard_map/while/body/eval_jaxpr/dot_general | solution.py:42
  253.0 3.3 %fusion.17 = f32[256,512]{1,0:T(8,128)S(1)} fusion(f32[2,1024,512]{2,1,0:T(8,128)S(1)} %get-tuple-element.347, f32[256,8192]{1,0:T(8,128)} %get-tuple-element.389, s32[]{:T(128)S(6)} %select_n.28, f32[256,512]{1,0:T(8,128)S(1)} %get-tuple-element.366, pred[]{:T(512)S(6)} %compare.3), kind=kOutput, calls=%fused_computation.9.clone.1 | convolution fusion | flops 1610874880 | bytes 4194309 | tf_op jit(solution)/shard_map/while/body/eval_jaxpr/dot_general | solution.py:45
  256.3 3.3 %fusion.16 = f32[256,512]{1,0:T(8,128)S(1)} fusion(f32[2,1024,512]{2,1,0:T(8,128)S(1)} %get-tuple-element.347, f32[256,8192]{1,0:T(8,128)} %get-tuple-element.383, s32[]{:T(128)S(6)} %select_n.28, f32[256,512]{1,0:T(8,128)S(1)} %get-tuple-element.365, pred[]{:T(512)S(6)} %compare.3), kind=kOutput, calls=%fused_computation.8.clone.1 | convolution fusion | flops 1610874880 | bytes 4194309 | tf_op jit(solution)/shard_map/while/body/eval_jaxpr/dot_general | solution.py:42
  261.5 3.3 %fusion.17 = f32[256,512]{1,0:T(8,128)S(1)} fusion(f32[2,1024,512]{2,1,0:T(8,128)S(1)} %get-tuple-element.347, f32[256,8192]{1,0:T(8,128)} %get-tuple-element.389, s32[]{:T(128)S(6)} %select_n.28, f32[256,512]{1,0:T(8,128)S(1)} %get-tuple-element.366, pred[]{:T(512)S(6)} %compare.3), kind=kOutput, calls=%fused_computation.9.clone.1 | convolution fusion | flops 1610874880 | bytes 4194309 | tf_op jit(solution)/shard_map/while/body/eval_jaxpr/dot_general | solution.py:45
  264.8 3.3 %fusion.16 = f32[256,512]{1,0:T(8,128)S(1)} fusion(f32[2,1024,512]{2,1,0:T(8,128)S(1)} %get-tuple-element.347, f32[256,8192]{1,0:T(8,128)} %get-tuple-element.383, s32[]{:T(128)S(6)} %select_n.28, f32[256,512]{1,0:T(8,128)S(1)} %get-tuple-element.365, pred[]{:T(512)S(6)} %compare.3), kind=kOutput, calls=%fused_computation.8.clone.1 | convolution fusion | flops 1610874880 | bytes 4194309 | tf_op jit(solution)/shard_map/while/body/eval_jaxpr/dot_general | solution.py:42
  270.1 3.3 %fusion.17 = f32[256,512]{1,0:T(8,128)S(1)} fusion(f32[2,1024,512]{2,1,0:T(8,128)S(1)} %get-tuple-element.347, f32[256,8192]{1,0:T(8,128)} %get-tuple-element.389, s32[]{:T(128)S(6)} %select_n.28, f32[256,512]{1,0:T(8,128)S(1)} %get-tuple-element.366, pred[]{:T(512)S(6)} %compare.3), kind=kOutput, calls=%fused_computation.9.clone.1 | convolution fusion | flops 1610874880 | bytes 4194309 | tf_op jit(solution)/shard_map/while/body/eval_jaxpr/dot_general | solution.py:45
  273.3 3.3 %fusion.16 = f32[256,512]{1,0:T(8,128)S(1)} fusion(f32[2,1024,512]{2,1,0:T(8,128)S(1)} %get-tuple-element.347, f32[256,8192]{1,0:T(8,128)} %get-tuple-element.383, s32[]{:T(128)S(6)} %select_n.28, f32[256,512]{1,0:T(8,128)S(1)} %get-tuple-element.365, pred[]{:T(512)S(6)} %compare.3), kind=kOutput, calls=%fused_computation.8.clone.1 | convolution fusion | flops 1610874880 | bytes 4194309 | tf_op jit(solution)/shard_map/while/body/eval_jaxpr/dot_general | solution.py:42
  278.6 3.3 %fusion.17 = f32[256,512]{1,0:T(8,128)S(1)} fusion(f32[2,1024,512]{2,1,0:T(8,128)S(1)} %get-tuple-element.347, f32[256,8192]{1,0:T(8,128)} %get-tuple-element.389, s32[]{:T(128)S(6)} %select_n.28, f32[256,512]{1,0:T(8,128)S(1)} %get-tuple-element.366, pred[]{:T(512)S(6)} %compare.3), kind=kOutput, calls=%fused_computation.9.clone.1 | convolution fusion | flops 1610874880 | bytes 4194309 | tf_op jit(solution)/shard_map/while/body/eval_jaxpr/dot_general | solution.py:45
  281.9 3.3 %fusion.16 = f32[256,512]{1,0:T(8,128)S(1)} fusion(f32[2,1024,512]{2,1,0:T(8,128)S(1)} %get-tuple-element.347, f32[256,8192]{1,0:T(8,128)} %get-tuple-element.383, s32[]{:T(128)S(6)} %select_n.28, f32[256,512]{1,0:T(8,128)S(1)} %get-tuple-element.365, pred[]{:T(512)S(6)} %compare.3), kind=kOutput, calls=%fused_computation.8.clone.1 | convolution fusion | flops 1610874880 | bytes 4194309 | tf_op jit(solution)/shard_map/while/body/eval_jaxpr/dot_general | solution.py:42
  287.1 15.6 %psum.7 = f32[512]{0:T(512)S(1)} all-reduce(f32[512]{0:T(512)S(1)} %get-tuple-element.266), channel_id=1, replica_groups=mesh['row'=8,'col'=32] {'row'}, use_global_device_ids=true, to_apply=%region_4.5 | all-reduce | flops 512 | bytes 4096 | tf_op jit(solution)/shard_map/psum | solution.py:59
  (59 shorter events, 17.4 us)
Async XLA Ops:
  7.2 106.8 %all-gather.3.cloned.1.call-start = ((), (), s32[]{:S(2)}) async-start(), calls=%async_computation | async-start | bytes 8650752 | tf_op jit(solution)/shard_map/all_gather | solution.py:26
  7.9 209.0 %all-gather.5.cloned.1.call-start = ((), (), s32[]{:S(2)}) async-start(), calls=%async_computation.1 | async-start | bytes 8650752 | tf_op jit(solution)/shard_map/all_gather | solution.py:27
Sparse Core Ops, SparseCore 0:
  10.4 103.4 all-gather.2
  116.4 100.4 all-gather.4
where the time goes:
time: 311 us; the launch traced here: 310 us
  waiting for transfers between devices  127 us (41%)
  blocking collectives  96.3 us (31%)
  matrix products  52.1 us (17%)
  other arithmetic  19.7 us (6%)
  between operations  14.1 us (5%)
    all_gather x1, waiting for transfers between devices, local(): lax.all_gather(lower_panel, 'col', axis=1, tiled=True)  103 us
    all_gather x1, blocking collectives, local(): lax.all_gather(weighted, 'col', axis=1, tiled=True)  41.5 us
    all_gather x1, blocking collectives, local(): lax.all_gather(pole_values, 'col', axis=1, tiled=True)  39.2 us
    dot_general x8, matrix products, advance(): jnp.dot(window[0], basis_tile[0], precision=exact_mode, preferred_element...  26 us
    dot_general x8, matrix products, advance(): jnp.dot(window[1], basis_tile[1], precision=exact_mode, preferred_element...  26 us
    all_gather x1, waiting for transfers between devices, local(): lax.all_gather(upper_panel, 'col', axis=1, tiled=True)  23.1 us
    psum x1, blocking collectives, local(): lax.psum(partial_weight, 'row') / (2 * rows_here * lax.axis_size('row'))  15.6 us
    reduce_sum x8, other arithmetic, advance(): jnp.sum(cauchy * cauchy, axis=(0, 1))  15 us
  transfers between devices with their start and end apart: 2, of which 2 were waited for; matrix products, arithmetic and copies ran while one was open for 0% of the time, Pallas kernels for 0%

commit v1 on v0

v1 whole, which is shorter than its diff:
```python
import functools

import jax
import jax.numpy as jnp
from jax import lax
from jax.experimental import pallas as pl
from jax.experimental.pallas import tpu as pltpu
from jax.sharding import PartitionSpec as P

NZ = 8
NY = 4
CHUNKS = 8
LEAD = 2
MESH = pl.DeviceIdType.MESH


def link(src, dst, ssem, rsem, dev):
    return pltpu.make_async_remote_copy(
        src_ref=src, dst_ref=dst, send_sem=ssem, recv_sem=rsem, device_id=dev, device_id_type=MESH
    )


def kernel(
    n_row, child_poles,
    up, lo, poles, coup, mask, shifts, source,
    out, slab,
    abuf, ahl, bh, bl, pbuf, rbuf, fbuf, xbuf, outv,
    pwbuf, ssbuf, nsend, nbuf, pcol, wcol, scale, sq, wbuf,
    own_l, own_s, own_r, s1, a1, sf, af, pws, pwr, sss, ssr, ns, nr,
    rls, rlr, fs, fr, xs, xr, ws, wr, osem,
):
    r = lax.axis_index("row")
    c = lax.axis_index("col")
    k = lax.rem(r, 2)
    r0 = r - k
    y = lax.div(c, NZ)
    z = lax.rem(c, NZ)
    nm = CHUNKS
    half = up.shape[1]
    kb = up.shape[2]
    m2 = 2 * half
    nc = shifts.shape[1]

    def at_z(delta, core):
        return (r0 + core, y * NZ + lax.rem(z + delta + NZ, NZ))

    def at_y(delta, core):
        return (r0 + core, lax.rem(y + delta + NY, NY) * NZ + z)

    def at_row(delta):
        return (lax.rem(r + delta, n_row), c)

    other = (r0 + 1 - k, c)

    barrier = pltpu.get_barrier_semaphore()
    peers = [at_z(d, k) for d in range(1, NZ)] + [at_z(1, 1 - k), at_z(NZ - 1, 1 - k)]
    peers += [at_y(d, q) for d in range(1, NY) for q in (0, 1)]
    peers += [at_row(d) for d in range(1, n_row)]
    for dev in peers:
        pl.semaphore_signal(barrier, inc=1, device_id=dev, device_id_type=MESH)

    pw_rows = lax.broadcasted_iota(jnp.int32, (8, kb), 0)
    pole_row = jnp.broadcast_to(poles[pl.ds(k, 1), :], (8, kb))
    weight_row = jnp.broadcast_to(
        coup[pl.ds(k, 1), :] * mask[pl.ds(k, 1), :].astype(jnp.float32), (8, kb)
    )
    pwbuf[0] = jnp.where(pw_rows == 0, pole_row, weight_row)
    ssbuf[0, 0] = jnp.broadcast_to(shifts[...], (8, nc))
    ssbuf[0, 1] = jnp.broadcast_to(source[...].astype(jnp.float32), (8, nc))
    nsend[...] = jnp.zeros_like(nsend)
    sq[...] = jnp.zeros_like(sq)

    pl.semaphore_wait(barrier, len(peers))

    panels = (up, lo)

    def own_copies(m):
        return [
            link(
                panels[child].at[m], abuf.at[NZ - 1 if step == 1 else 1, m, k],
                s1.at[d, m, child], a1.at[d, m, k], at_z(step, child),
            )
            for d, step in ((0, 1), (1, NZ - 1))
            for child in (0, 1)
        ]

    def first_wait(d, m, o):
        dst = abuf.at[NZ - 1 if d == 0 else 1, m, o]
        return link(dst, dst, s1.at[d, m, 0], a1.at[d, m, o], other)

    def forward(d, m, stage):
        step = 1 if d == 0 else NZ - 1
        src_rel = NZ - 1 - stage if d == 0 else 1 + stage
        dst_rel = src_rel - 1 if d == 0 else src_rel + 1
        if stage < 2:
            src, dst = abuf.at[src_rel, m], abuf.at[dst_rel, m]
        else:
            src, dst = abuf.at[src_rel, m, d], abuf.at[dst_rel, m, d]
        return link(src, dst, sf.at[d, m, stage], af.at[d, m, stage], at_z(step, k))

    for dlt in range(1, NZ):
        link(pwbuf.at[0], pwbuf.at[NZ - dlt], pws.at[dlt], pwr.at[NZ - dlt], at_z(dlt, k)).start()
    for dlt in range(1, NY):
        link(ssbuf.at[0], ssbuf.at[NY - dlt], sss.at[dlt], ssr.at[NY - dlt], at_y(dlt, k)).start()
    for m in range(LEAD + 1):
        for copy in own_copies(m):
            copy.start()
    for child in (0, 1):
        local = pltpu.make_async_copy(panels[child], abuf.at[0, :, k], own_l)
        across = link(panels[child], abuf.at[0, :, k], own_s, own_r, other)

        @pl.when(k == child)
        def _():
            local.start()

        @pl.when(k != child)
        def _():
            across.start()

    for dlt in range(1, NY):
        link(ssbuf.at[0], ssbuf.at[dlt], sss.at[dlt], ssr.at[dlt], other).wait_recv()
    for dlt in range(1, NZ):
        link(pwbuf.at[0], pwbuf.at[dlt], pws.at[dlt], pwr.at[dlt], other).wait_recv()

    block_rows = min(64, kb)

    def basis_block(rel):
        pw = pwbuf[rel]
        pcol[...] = jnp.broadcast_to(pw[0:1, :], (128, kb)).T
        wcol[...] = jnp.broadcast_to(pw[1:2, :], (128, kb)).T
        first = k * child_poles + (y * NZ + lax.rem(z + rel, NZ)) * kb

        @pl.loop(0, NY * (nc // 128))
        def _(tile):
            dest = lax.div(tile, nc // 128)
            lane = pl.multiple_of(lax.rem(tile, nc // 128) * 128, 128)
            shift = ssbuf[dest, 0, :, pl.ds(lane, 128)]
            named = ssbuf[dest, 1, :, pl.ds(lane, 128)]
            kept = named == 2.0 * child_poles
            total = nsend[dest, :, pl.ds(lane, 128)]
            for rb in range(kb // block_rows):
                rows = pl.ds(rb * block_rows, block_rows)
                shape = (block_rows // 8, 8, 128)
                pole = pcol[rows, :].reshape(shape)
                weight = wcol[rows, :].reshape(shape)
                cauchy = weight / (pole - shift[None])
                total = total + jnp.sum(cauchy * cauchy, axis=0)
                ids = (
                    lax.broadcasted_iota(jnp.int32, shape, 0) * 8
                    + lax.broadcasted_iota(jnp.int32, shape, 1)
                    + (first + rb * block_rows)
                ).astype(jnp.float32)
                hot = jnp.where(ids == named[None], 1.0, 0.0)
                value = jnp.where(kept[None], cauchy, hot).reshape(block_rows, 128)
                high = value.astype(jnp.bfloat16)
                low = (value - high.astype(jnp.float32)).astype(jnp.bfloat16)
                at = pl.ds(pl.multiple_of(rel * kb + rb * block_rows, block_rows), block_rows)
                bh[dest, at, pl.ds(lane, 128)] = high
                bl[dest, at, pl.ds(lane, 128)] = low
            nsend[dest, :, pl.ds(lane, 128)] = total

    def norm_copies():
        copies = []
        for dlt in range(NY):
            for q in (0, 1):
                slot = (NY - dlt) % NY
                copies.append((dlt, q, link(
                    nsend.at[dlt], nbuf.at[slot, k], ns.at[dlt, q], nr.at[slot, k], at_y(dlt, q)
                )))
        return copies

    def relay(m, d):
        step = 1 if d == 0 else NY - 1
        return link(pbuf.at[2, m, d], rbuf.at[d, m], rls.at[d, m], rlr.at[d, m], at_y(step, k))

    def final(m, d, o):
        step = 1 if d == 0 else NY - 1
        return link(
            pbuf.at[step, m, o], fbuf.at[k, d, m], fs.at[d, m, o], fr.at[k, d, m], at_y(step, o)
        )

    def cross(m):
        return link(pbuf.at[0, m, 1 - k], xbuf.at[m], xs.at[m], xr.at[m], other)

    def multiply(m):
        for rel in range(NZ):
            a = abuf[rel, m].reshape(m2, kb)
            high = a.astype(jnp.bfloat16)
            low = (a - high.astype(jnp.float32)).astype(jnp.bfloat16)
            ahl[0:m2, rel * kb : (rel + 1) * kb] = high
            ahl[m2 : 2 * m2, rel * kb : (rel + 1) * kb] = low
        for dest in (2, 1, 3, 0):
            both = jnp.dot(ahl[...], bh[dest], preferred_element_type=jnp.float32)
            rest = jnp.dot(ahl[0:m2, :], bl[dest], preferred_element_type=jnp.float32)
            pbuf[dest, m] = (both[0:m2] + (both[m2:] + rest)).reshape(2, half, nc)
            if dest == 2:
                relay(m, 0).start()
                relay(m, 1).start()
            elif dest == 1:
                final(m, 0, 1).start()
            elif dest == 3:
                final(m, 1, 0).start()
            else:
                cross(m).start()

    def add_relays(m):
        relay(m, 0).wait_recv()
        pbuf[1, m, 0] = pbuf[1, m, 0] + rbuf[0, m]
        final(m, 0, 0).start()
        relay(m, 1).wait_recv()
        pbuf[3, m, 1] = pbuf[3, m, 1] + rbuf[1, m]
        final(m, 1, 1).start()

    def finish(m):
        for child in (0, 1):
            for d in (0, 1):
                dst = fbuf.at[child, d, m]
                link(dst, dst, fs.at[d, m, 0], fr.at[child, d, m], other).wait_recv()
        cross(m).wait_recv()
        factor = scale[0:1, :]
        mine = (pbuf[0, m, k] + (fbuf[k, 0, m] + fbuf[k, 1, m])) * factor
        theirs = (xbuf[m] + (fbuf[1 - k, 0, m] + fbuf[1 - k, 1, m])) * factor
        outv[k, m] = mine
        outv[1 - k, m] = theirs
        squares = (mine * mine + theirs * theirs).reshape(half // 8, 8, nc)
        sq[...] = sq[...] + jnp.sum(squares, axis=0)
        pltpu.make_async_copy(outv.at[:, m], out.at[:, m], osem.at[m]).start()

    def within(m):
        return jnp.logical_and(m >= 0, m < nm)

    @pl.loop(0, nm + 6)
    def _(t):
        @pl.when(within(t - 4))
        def _():
            for d in (0, 1):
                forward(d, t - 4, 2).wait_recv()

        for stage in (2, 1):
            @pl.when(within(t - 1 - stage))
            def _():
                for d in (0, 1):
                    forward(d, t - 1 - stage, stage - 1).wait_recv()
                    forward(d, t - 1 - stage, stage).start()

        @pl.when(within(t - 1))
        def _():
            for d in (0, 1):
                for o in (0, 1):
                    first_wait(d, t - 1, o).wait_recv()
                forward(d, t - 1, 0).start()

        @pl.when(t + LEAD + 1 < nm)
        def _():
            for copy in own_copies(t + LEAD + 1):
                copy.start()

        @pl.when(t < 4)
        def _():
            basis_block(2 * t)
            basis_block(2 * t + 1)

        @pl.when(t == 3)
        def _():
            pltpu.make_async_copy(up, abuf.at[0, :, k], own_l).wait()
            link(up, abuf.at[0, :, 1 - k], own_s, own_r, other).wait_recv()
            for dlt, q, copy in norm_copies():
                if dlt > 0:
                    copy.start()
                else:
                    @pl.when(k != q)
                    def _():
                        copy.start()
            nbuf[0, k] = nsend[0]

        @pl.when(within(t - 4))
        def _():
            multiply(t - 4)

        @pl.when(within(t - 5))
        def _():
            add_relays(t - 5)

        @pl.when(t == 6)
        def _():
            total = jnp.zeros((8, nc), jnp.float32)
            for slot in range(NY):
                for q in (0, 1):
                    dst = nbuf.at[slot, q]
                    incoming = link(dst, dst, ns.at[1, 0], nr.at[slot, q], other)
                    if slot > 0:
                        incoming.wait_recv()
                    else:
                        @pl.when(k != q)
                        def _():
                            incoming.wait_recv()
            for slot in range(NY):
                for q in (0, 1):
                    total = total + nbuf[slot, q]
            sums = jnp.sum(total, axis=0, keepdims=True)
            kept = ssbuf[0, 1, 0:1, :] == 2.0 * child_poles
            scale[...] = jnp.broadcast_to(
                jnp.where(kept, 1.0 / jnp.sqrt(sums), 1.0), (8, nc)
            )

        @pl.when(within(t - 6))
        def _():
            finish(t - 6)

    wbuf[0] = sq[...]
    for dlt in range(1, n_row):
        link(wbuf.at[0], wbuf.at[n_row - dlt], ws.at[dlt], wr.at[n_row - dlt], at_row(dlt)).start()

    for dlt in range(1, NZ):
        link(pwbuf.at[0], pwbuf.at[dlt], pws.at[dlt], pwr.at[dlt], other).wait_send()
    for dlt in range(1, NY):
        link(ssbuf.at[0], ssbuf.at[dlt], sss.at[dlt], ssr.at[dlt], other).wait_send()
    link(up, abuf.at[0, :, k], own_s, own_r, other).wait_send()
    for dlt, q, copy in norm_copies():
        if dlt > 0:
            copy.wait_send()
        else:
            @pl.when(k != q)
            def _():
                copy.wait_send()

    @pl.loop(0, nm)
    def _(m):
        for copy in own_copies(m):
            copy.wait_send()
        for d in (0, 1):
            for stage in (0, 1, 2):
                forward(d, m, stage).wait_send()
            relay(m, d).wait_send()
            final(m, d, 0).wait_send()
            final(m, d, 1).wait_send()
        cross(m).wait_send()
        pltpu.make_async_copy(outv.at[:, m], out.at[:, m], osem.at[m]).wait()

    weight_sum = wbuf[0]
    for dlt in range(1, n_row):
        link(wbuf.at[0], wbuf.at[dlt], ws.at[dlt], wr.at[dlt], other).wait_recv()
    for dlt in range(1, n_row):
        weight_sum = weight_sum + wbuf[dlt]
    rows_all = 2 * n_row * nm * half
    slab[...] = jnp.sum(weight_sum, axis=0, keepdims=True) * (1.0 / rows_all)
    for dlt in range(1, n_row):
        link(wbuf.at[0], wbuf.at[dlt], ws.at[dlt], wr.at[dlt], other).wait_send()


def local(n_row, upper_panel, lower_panel, pole_values, coupling, kept_mask, shifts, source):
    rows, kb = upper_panel.shape
    nc = shifts.shape[0]
    nm = CHUNKS
    half = rows // nm
    m2 = 2 * half
    child_poles = NZ * NY * kb
    kpart = NZ * kb
    f32 = jnp.float32
    dma = pltpu.SemaphoreType.DMA
    vmem = pl.BlockSpec(memory_space=pltpu.VMEM)
    hbm = pl.BlockSpec(memory_space=pl.ANY)
    out, slab = pl.pallas_call(
        functools.partial(kernel, n_row, child_poles),
        out_shape=(
            jax.ShapeDtypeStruct((2, nm, half, nc), f32),
            jax.ShapeDtypeStruct((1, nc), f32),
        ),
        in_specs=[hbm, hbm, vmem, vmem, vmem, vmem, vmem],
        out_specs=(hbm, vmem),
        scratch_shapes=[
            pltpu.VMEM((NZ, nm, 2, half, kb), f32),
            pltpu.VMEM((2 * m2, kpart), jnp.bfloat16),
            pltpu.VMEM((NY, kpart, nc), jnp.bfloat16),
            pltpu.VMEM((NY, kpart, nc), jnp.bfloat16),
            pltpu.VMEM((NY, nm, 2, half, nc), f32),
            pltpu.VMEM((2, nm, half, nc), f32),
            pltpu.VMEM((2, 2, nm, half, nc), f32),
            pltpu.VMEM((nm, half, nc), f32),
            pltpu.VMEM((2, nm, half, nc), f32),
            pltpu.VMEM((NZ, 8, kb), f32),
            pltpu.VMEM((NY, 2, 8, nc), f32),
            pltpu.VMEM((NY, 8, nc), f32),
            pltpu.VMEM((NY, 2, 8, nc), f32),
            pltpu.VMEM((kb, 128), f32),
            pltpu.VMEM((kb, 128), f32),
            pltpu.VMEM((8, nc), f32),
            pltpu.VMEM((8, nc), f32),
            pltpu.VMEM((n_row, 8, nc), f32),
            dma, dma, dma,
            dma((2, nm, 2)), dma((2, nm, 2)),
            dma((2, nm, 3)), dma((2, nm, 3)),
            dma((NZ,)), dma((NZ,)),
            dma((NY,)), dma((NY,)),
            dma((NY, 2)), dma((NY, 2)),
            dma((2, nm)), dma((2, nm)),
            dma((2, nm, 2)), dma((2, 2, nm)),
            dma((nm,)), dma((nm,)),
            dma((n_row,)), dma((n_row,)),
            dma((nm,)),
        ],
        compiler_params=pltpu.CompilerParams(
            collective_id=0, has_side_effects=True, vmem_limit_bytes=60 * 1024 * 1024
        ),
    )(
        upper_panel.reshape(nm, half, kb),
        lower_panel.reshape(nm, half, kb),
        pole_values,
        coupling,
        kept_mask,
        shifts.reshape(1, nc),
        source.reshape(1, nc),
    )
    return out.reshape(2, rows, nc), slab.reshape(nc)


def solution(mesh):
    in_specs = (
        P("row", "col"),
        P("row", "col"),
        P(None, "col"),
        P(None, "col"),
        P(None, "col"),
        P("col"),
        P("col"),
    )
    out_specs = (P(None, "row", "col"), P("col"))
    body = functools.partial(local, mesh.shape["row"])
    return jax.shard_map(body, mesh=mesh, in_specs=in_specs, out_specs=out_specs, check_vma=False)
```

time: 311 us -> 86.5 us (0.28)
  waiting for transfers between devices: 127 us -> 0 us
  blocking collectives: 96.3 us -> 0 us
  Pallas kernels: 0 us -> 82.9 us
  matrix products: 52.1 us -> 0 us
  other arithmetic: 19.7 us -> 0 us
  between operations: 14.1 us -> 0.65 us
    all_gather x2 -> x0, waiting for transfers between devices: 126 us -> none  [the longest x1 103 us: local(): lax.all_gather(lower_panel, 'col', axis=1, tiled=True)]
    pallas_call x0 -> x1, Pallas kernels: none -> 82.9 us  [local(): pl.pallas_call(functools.partial(kernel, n_row, child_poles), out_shape=(...]
    all_gather x2 -> x0, blocking collectives: 80.7 us -> none  [the longest x1 41.5 us: local(): lax.all_gather(weighted, 'col', axis=1, tiled=True)]
    dot_general x16 -> x0, matrix products: 52.1 us -> none  [the longest x8 26 us: advance(): jnp.dot(window[0], basis_tile[0], precision=exact_mode, preferred_element...]
    reduce_sum x9 -> x0, other arithmetic: 16.1 us -> none  [the longest x8 15 us: advance(): jnp.sum(cauchy * cauchy, axis=(0, 1))]
    psum x1 -> x0, blocking collectives: 15.6 us -> none  [local(): lax.psum(partial_weight, 'row') / (2 * rows_here * lax.axis_size('row'))]
  transfers between devices with their start and end apart: 2 -> 0, of which waited for: 2 -> 0; matrix products, arithmetic and copies ran while one was open for 0% -> 0% of each run, Pallas kernels for 0% -> 0%
where the time goes in v1:
time: 86.5 us; the launch traced here: 86.3 us
  Pallas kernels  82.9 us (96%)
  local copies, waits for them, and re-layouts  2.85 us (3%)
    pallas_call x1, Pallas kernels, local(): pl.pallas_call(functools.partial(kernel, n_row, child_poles), out_shape=(...  82.9 us
    unnamed x4, local copies, waits for them, and re-layouts  2.85 us

profile of v1, /device:TPU:1, one launch (start us, length us, event | category | flops | bytes accessed | tf_op | source)
XLA Modules:
  0.0 86.3 jit_solution(16227939420228571500)
XLA Ops:
  0.6 82.9 %shard_map.86 = (f32[2,8,32,512]{3,2,1,0:T(8,128)}, f32[1,512]{1,0:T(1,128)}) custom-call(f32[8,32,256]{2,1,0:T(8,128)} %bitcast.7, f32[8,32,256]{2,1,0:T(8,128)} %bitcast.8, f32[2,256]{1,0:T(2,128)} %poles.1, f32[2,256]{1,0:T(2,128)} %coup.1, s32[2,256]{1,0:T(2,128)} %mask.1, f32[1,512]{1,0:T(1,128)} %bitcast.9, s32[1,512]{1,0:T(1,128)} %bitcast.10), custom_call_target="tpu_custom_call" | custom-call | tf_op jit(solution)/shard_map/pallas_call | solution.py:363
  83.5 0.0 copy-start
  83.5 2.3 %copy.11 = f32[2,256,512]{2,1,0:T(8,128)} copy(f32[2,256,512]{2,1,0:T(8,128)} %bitcast.6) | data formatting | bytes 2097152
  85.8 0.0 copy-done
  85.8 0.6 copy.12
Async XLA Ops:
  83.5 2.3 %copy-start = (f32[1,512]{1,0:T(1,128)S(1)}, f32[1,512]{1,0:T(1,128)}, u32[]{:S(2)}) copy-start(f32[1,512]{1,0:T(1,128)} %get-tuple-element.5) | copy-start | bytes 6148

commit v2 on v1

v2 whole, which is shorter than its diff:
```python
import functools

import jax
import jax.numpy as jnp
from jax import lax
from jax.experimental import pallas as pl
from jax.experimental.pallas import tpu as pltpu
from jax.sharding import PartitionSpec as P

NZ = 8
NY = 4
CHUNKS = 8
LEAD = 3
MESH = pl.DeviceIdType.MESH


def link(src, dst, ssem, rsem, dev):
    return pltpu.make_async_remote_copy(
        src_ref=src, dst_ref=dst, send_sem=ssem, recv_sem=rsem, device_id=dev, device_id_type=MESH
    )


def kernel(
    n_row, child_poles,
    up, lo, poles, coup, mask, shifts, source,
    out, slab,
    abuf, ahl, atail, bh, bl, pbuf, rbuf, fbuf, outv,
    pwbuf, ssbuf, nsend, nbuf, pcol, wcol, scale, sq, wbuf,
    own_l, own_s, own_r, s1, a1, sf, af, pws, pwr, sss, ssr, ns, nr,
    rls, rlr, fs, fr, xs, ws, wr, osem,
):
    r = lax.axis_index("row")
    c = lax.axis_index("col")
    k = lax.rem(r, 2)
    r0 = r - k
    y = lax.div(c, NZ)
    z = lax.rem(c, NZ)
    nm = CHUNKS
    half = up.shape[1]
    kb = up.shape[2]
    m2 = 2 * half
    nc = shifts.shape[1]

    def at_z(delta, core):
        return (r0 + core, y * NZ + lax.rem(z + delta + NZ, NZ))

    def at_y(delta, core):
        return (r0 + core, lax.rem(y + delta + NY, NY) * NZ + z)

    def at_row(delta):
        return (lax.rem(r + delta, n_row), c)

    other = (r0 + 1 - k, c)

    barrier = pltpu.get_barrier_semaphore()
    peers = [at_z(d, k) for d in range(1, NZ)] + [at_z(1, 1 - k), at_z(NZ - 1, 1 - k)]
    peers += [at_y(d, q) for d in range(1, NY) for q in (0, 1)]
    peers += [at_row(d) for d in range(1, n_row)]
    for dev in peers:
        pl.semaphore_signal(barrier, inc=1, device_id=dev, device_id_type=MESH)

    pw_rows = lax.broadcasted_iota(jnp.int32, (8, kb), 0)
    pole_row = jnp.broadcast_to(poles[pl.ds(k, 1), :], (8, kb))
    weight_row = jnp.broadcast_to(
        coup[pl.ds(k, 1), :] * mask[pl.ds(k, 1), :].astype(jnp.float32), (8, kb)
    )
    pwbuf[0] = jnp.where(pw_rows == 0, pole_row, weight_row)
    ssbuf[0, 0] = jnp.broadcast_to(shifts[...], (8, nc))
    ssbuf[0, 1] = jnp.broadcast_to(source[...].astype(jnp.float32), (8, nc))
    nsend[...] = jnp.zeros_like(nsend)
    sq[...] = jnp.zeros_like(sq)

    pl.semaphore_wait(barrier, len(peers))

    panels = (up, lo)

    def own_copies(m):
        return [
            link(
                panels[child].at[m], abuf.at[NZ - 1 if step == 1 else 1, m, k],
                s1.at[d, lax.rem(m, 4), child], a1.at[d, m], at_z(step, child),
            )
            for d, step in ((0, 1), (1, NZ - 1))
            for child in (0, 1)
        ]

    def first_wait(d, m):
        dst = abuf.at[NZ - 1 if d == 0 else 1, m]
        return link(dst, dst, s1.at[d, 0, 0], a1.at[d, m], other)

    def forward(d, m, stage):
        step = 1 if d == 0 else NZ - 1
        src_rel = NZ - 1 - stage if d == 0 else 1 + stage
        dst_rel = src_rel - 1 if d == 0 else src_rel + 1
        if stage < 2:
            src, dst = abuf.at[src_rel, m], abuf.at[dst_rel, m]
        else:
            src, dst = abuf.at[src_rel, m, d], abuf.at[dst_rel, m, d]
        return link(src, dst, sf.at[d, lax.rem(m, 2), stage], af.at[d, m, stage], at_z(step, k))

    def push(d, m, stage):
        @pl.when(m >= 2)
        def _():
            forward(d, m - 2, stage).wait_send()

        forward(d, m, stage).start()

    for dlt in range(1, NZ):
        link(pwbuf.at[0], pwbuf.at[NZ - dlt], pws, pwr, at_z(dlt, k)).start()
    for dlt in range(1, NY):
        link(ssbuf.at[0], ssbuf.at[NY - dlt], sss, ssr, at_y(dlt, k)).start()
    for m in range(LEAD):
        for copy in own_copies(m):
            copy.start()
    for child in (0, 1):
        local = pltpu.make_async_copy(panels[child], abuf.at[0, :, k], own_l)
        across = link(panels[child], abuf.at[0, :, k], own_s, own_r, other)

        @pl.when(k == child)
        def _():
            local.start()

        @pl.when(k != child)
        def _():
            across.start()

    all_shifts = link(ssbuf.at[1:NY], ssbuf.at[1:NY], sss, ssr, other)
    all_poles = link(pwbuf.at[1:NZ], pwbuf.at[1:NZ], pws, pwr, other)
    all_shifts.wait_recv()
    block_rows = min(64, kb)

    def basis_block(pos):
        rel = pos + lax.div(pos, 4) - 4 * lax.div(pos, NZ - 1)
        pw = pwbuf[rel]
        pcol[...] = jnp.broadcast_to(pw[0:1, :], (128, kb)).T
        wcol[...] = jnp.broadcast_to(pw[1:2, :], (128, kb)).T
        first = k * child_poles + (y * NZ + lax.rem(z + rel, NZ)) * kb

        @pl.loop(0, NY * (nc // 128))
        def _(tile):
            dest = lax.div(tile, nc // 128)
            lane = pl.multiple_of(lax.rem(tile, nc // 128) * 128, 128)
            shift = ssbuf[dest, 0, :, pl.ds(lane, 128)]
            named = ssbuf[dest, 1, :, pl.ds(lane, 128)]
            kept = named == 2.0 * child_poles
            total = nsend[dest, :, pl.ds(lane, 128)]
            for rb in range(kb // block_rows):
                rows = pl.ds(rb * block_rows, block_rows)
                shape = (block_rows // 8, 8, 128)
                pole = pcol[rows, :].reshape(shape)
                weight = wcol[rows, :].reshape(shape)
                cauchy = weight / (pole - shift[None])
                total = total + jnp.sum(cauchy * cauchy, axis=0)
                ids = (
                    lax.broadcasted_iota(jnp.int32, shape, 0) * 8
                    + lax.broadcasted_iota(jnp.int32, shape, 1)
                    + (first + rb * block_rows)
                ).astype(jnp.float32)
                hot = jnp.where(ids == named[None], 1.0, 0.0)
                value = jnp.where(kept[None], cauchy, hot).reshape(block_rows, 128)
                high = value.astype(jnp.bfloat16)
                low = (value - high.astype(jnp.float32)).astype(jnp.bfloat16)
                at = pl.ds(pl.multiple_of(pos * kb + rb * block_rows, block_rows), block_rows)
                bh[dest, at, pl.ds(lane, 128)] = high
                bl[dest, at, pl.ds(lane, 128)] = low
            nsend[dest, :, pl.ds(lane, 128)] = total

    def send_norms():
        for dlt in range(NY):
            for flip in (0, 1):
                slot = 2 * ((NY - dlt) % NY) + flip
                if slot > 0:
                    core = 1 - k if flip else k
                    link(nsend.at[dlt], nbuf.at[slot], ns, nr, at_y(dlt, core)).start()

    all_norms = link(nbuf.at[1 : 2 * NY], nbuf.at[1 : 2 * NY], ns, nr, other)

    def relay(m, d):
        step = 1 if d == 0 else NY - 1
        return link(
            pbuf.at[2, m, d], rbuf.at[d, m], rls.at[d, lax.rem(m, 2)], rlr.at[d, m], at_y(step, k)
        )

    def final(m, d, o):
        step = 1 if d == 0 else NY - 1
        return link(
            pbuf.at[step, m, o], fbuf.at[m, 2 * k + d], fs.at[d, lax.rem(m, 2), o], fr.at[m],
            at_y(step, o),
        )

    def cross(m):
        return link(pbuf.at[0, m, 1 - k], fbuf.at[m, 4], xs.at[lax.rem(m, 2)], fr.at[m], other)

    def split(rel, m):
        a = abuf[rel, m].reshape(m2, kb)
        high = a.astype(jnp.bfloat16)
        return high, (a - high.astype(jnp.float32)).astype(jnp.bfloat16)

    def split_early(m):
        for pos in range(NZ - 1):
            high, low = split(pos + pos // 4, m)
            ahl[0:m2, pos * kb : (pos + 1) * kb] = high
            ahl[m2 : 2 * m2, pos * kb : (pos + 1) * kb] = low

    early = (NZ - 1) * kb

    def product(a, dest, first, size):
        rows = slice(first, first + size)
        both = jnp.dot(a[...], bh[dest, rows, :], preferred_element_type=jnp.float32)
        rest = jnp.dot(a[0:m2, :], bl[dest, rows, :], preferred_element_type=jnp.float32)
        return (both[0:m2] + (both[m2:] + rest)).reshape(2, half, nc)

    def multiply_early(m, dest):
        pbuf[dest, m] = product(ahl, dest, 0, early)

    def multiply_late(m):
        atail[0:m2, :], atail[m2 : 2 * m2, :] = split(4, m)
        for dest in (2, 1, 3, 0):
            pbuf[dest, m] = pbuf[dest, m] + product(atail, dest, early, kb)
            if dest == 2:
                relay(m, 0).start()
                relay(m, 1).start()
            elif dest == 1:
                final(m, 0, 1).start()
            elif dest == 3:
                final(m, 1, 0).start()
            else:
                cross(m).start()

    def sums_sent(m):
        for d in (0, 1):
            relay(m, d).wait_send()
            final(m, d, 1 - d).wait_send()
        cross(m).wait_send()

    def added_sent(m):
        for d in (0, 1):
            final(m, d, d).wait_send()

    def add_relays(m):
        @pl.when(m >= 2)
        def _():
            added_sent(m - 2)

        relay(m, 0).wait_recv()
        pbuf[1, m, 0] = pbuf[1, m, 0] + rbuf[0, m]
        final(m, 0, 0).start()
        relay(m, 1).wait_recv()
        pbuf[3, m, 1] = pbuf[3, m, 1] + rbuf[1, m]
        final(m, 1, 1).start()

    def store(m):
        return pltpu.make_async_copy(outv.at[:, m], out.at[:, m], osem.at[lax.rem(m, 2)])

    def finish(m):
        link(fbuf.at[m], fbuf.at[m], xs.at[0], fr.at[m], other).wait_recv()
        factor = scale[0:1, :]
        mine = (pbuf[0, m, k] + (fbuf[m, 2 * k] + fbuf[m, 2 * k + 1])) * factor
        theirs = (fbuf[m, 4] + (fbuf[m, 2 - 2 * k] + fbuf[m, 3 - 2 * k])) * factor
        outv[k, m] = mine
        outv[1 - k, m] = theirs
        squares = (mine * mine + theirs * theirs).reshape(half // 8, 8, nc)
        sq[...] = sq[...] + jnp.sum(squares, axis=0)
        @pl.when(m >= 2)
        def _():
            store(m - 2).wait()

        store(m).start()

    def within(m):
        return jnp.logical_and(m >= 0, m < nm)

    @pl.loop(0, nm + 6)
    def _(t):
        @pl.when(within(t - 4))
        def _():
            for d in (0, 1):
                forward(d, t - 4, 2).wait_recv()
            @pl.when(t >= 6)
            def _():
                sums_sent(t - 6)
            multiply_late(t - 4)

        @pl.when(t + LEAD < nm)
        def _():
            @pl.when(t + LEAD >= 4)
            def _():
                for copy in own_copies(t + LEAD - 4):
                    copy.wait_send()
            for copy in own_copies(t + LEAD):
                copy.start()

        @pl.when(t < 3)
        def _():
            basis_block(3 * t)

        @pl.when(t == 0)
        def _():
            all_poles.wait_recv()

        @pl.when(within(t))
        def _():
            for d in (0, 1):
                first_wait(d, t).wait_recv()
                push(d, t, 0)

        @pl.when(t < 3)
        def _():
            basis_block(3 * t + 1)

        @pl.when(within(t - 3))
        def _():
            split_early(t - 3)
            multiply_early(t - 3, 2)

        @pl.when(within(t - 1))
        def _():
            for d in (0, 1):
                forward(d, t - 1, 0).wait_recv()
                push(d, t - 1, 1)

        @pl.when(t < 2)
        def _():
            basis_block(3 * t + 2)

        @pl.when(within(t - 3))
        def _():
            multiply_early(t - 3, 1)

        @pl.when(within(t - 2))
        def _():
            for d in (0, 1):
                forward(d, t - 2, 1).wait_recv()
                push(d, t - 2, 2)

        @pl.when(within(t - 3))
        def _():
            multiply_early(t - 3, 3)
            multiply_early(t - 3, 0)

        @pl.when(t == 2)
        def _():
            pltpu.make_async_copy(up, abuf.at[0, :, k], own_l).wait()
            link(up, abuf.at[0, :, 1 - k], own_s, own_r, other).wait_recv()
            send_norms()
            nbuf[0] = nsend[0]

        @pl.when(within(t - 5))
        def _():
            add_relays(t - 5)

        @pl.when(t == 6)
        def _():
            all_norms.wait_recv()
            total = nbuf[0]
            for slot in range(1, 2 * NY):
                total = total + nbuf[slot]
            sums = jnp.sum(total, axis=0, keepdims=True)
            kept = ssbuf[0, 1, 0:1, :] == 2.0 * child_poles
            scale[...] = jnp.broadcast_to(
                jnp.where(kept, 1.0 / jnp.sqrt(sums), 1.0), (8, nc)
            )

        @pl.when(within(t - 6))
        def _():
            finish(t - 6)

    wbuf[0] = jnp.sum(sq[...], axis=0, keepdims=True)
    for dlt in range(1, n_row):
        link(wbuf.at[0], wbuf.at[n_row - dlt], ws, wr, at_row(dlt)).start()
    all_weights = link(wbuf.at[1:n_row], wbuf.at[1:n_row], ws, wr, other)

    all_poles.wait_send()
    all_shifts.wait_send()
    link(up, abuf.at[0, :, k], own_s, own_r, other).wait_send()
    all_norms.wait_send()

    for m in range(nm - 4, nm):
        for copy in own_copies(m):
            copy.wait_send()
    for m in range(nm - 2, nm):
        for d in (0, 1):
            for stage in (0, 1, 2):
                forward(d, m, stage).wait_send()
        sums_sent(m)
        added_sent(m)
        store(m).wait()

    weight_sum = wbuf[0]
    all_weights.wait_recv()
    for dlt in range(1, n_row):
        weight_sum = weight_sum + wbuf[dlt]
    rows_all = 2 * n_row * nm * half
    slab[...] = weight_sum * (1.0 / rows_all)
    all_weights.wait_send()


def local(n_row, upper_panel, lower_panel, pole_values, coupling, kept_mask, shifts, source):
    rows, kb = upper_panel.shape
    nc = shifts.shape[0]
    nm = CHUNKS
    half = rows // nm
    m2 = 2 * half
    child_poles = NZ * NY * kb
    kpart = NZ * kb
    f32 = jnp.float32
    dma = pltpu.SemaphoreType.DMA
    vmem = pl.BlockSpec(memory_space=pltpu.VMEM)
    hbm = pl.BlockSpec(memory_space=pl.ANY)
    out, slab = pl.pallas_call(
        functools.partial(kernel, n_row, child_poles),
        out_shape=(
            jax.ShapeDtypeStruct((2, nm, half, nc), f32),
            jax.ShapeDtypeStruct((1, nc), f32),
        ),
        in_specs=[hbm, hbm, vmem, vmem, vmem, vmem, vmem],
        out_specs=(hbm, vmem),
        scratch_shapes=[
            pltpu.VMEM((NZ, nm, 2, half, kb), f32),
            pltpu.VMEM((2 * m2, kpart - kb), jnp.bfloat16),
            pltpu.VMEM((2 * m2, kb), jnp.bfloat16),
            pltpu.VMEM((NY, kpart, nc), jnp.bfloat16),
            pltpu.VMEM((NY, kpart, nc), jnp.bfloat16),
            pltpu.VMEM((NY, nm, 2, half, nc), f32),
            pltpu.VMEM((2, nm, half, nc), f32),
            pltpu.VMEM((nm, 5, half, nc), f32),
            pltpu.VMEM((2, nm, half, nc), f32),
            pltpu.VMEM((NZ, 8, kb), f32),
            pltpu.VMEM((NY, 2, 8, nc), f32),
            pltpu.VMEM((NY, 8, nc), f32),
            pltpu.VMEM((2 * NY, 8, nc), f32),
            pltpu.VMEM((kb, 128), f32),
            pltpu.VMEM((kb, 128), f32),
            pltpu.VMEM((8, nc), f32),
            pltpu.VMEM((8, nc), f32),
            pltpu.VMEM((n_row, 1, nc), f32),
            dma, dma, dma,
            dma((2, 4, 2)), dma((2, nm)),
            dma((2, 2, 3)), dma((2, nm, 3)),
            dma, dma, dma, dma, dma, dma,
            dma((2, 2)), dma((2, nm)),
            dma((2, 2, 2)), dma((nm,)),
            dma((2,)), dma, dma, dma((2,)),
        ],
        compiler_params=pltpu.CompilerParams(
            collective_id=0, has_side_effects=True, vmem_limit_bytes=60 * 1024 * 1024
        ),
    )(
        upper_panel.reshape(nm, half, kb),
        lower_panel.reshape(nm, half, kb),
        pole_values,
        coupling,
        kept_mask,
        shifts.reshape(1, nc),
        source.reshape(1, nc),
    )
    return out.reshape(2, rows, nc), slab.reshape(nc)


def solution(mesh):
    in_specs = (
        P("row", "col"),
        P("row", "col"),
        P(None, "col"),
        P(None, "col"),
        P(None, "col"),
        P("col"),
        P("col"),
    )
    out_specs = (P(None, "row", "col"), P("col"))
    body = functools.partial(local, mesh.shape["row"])
    return jax.shard_map(body, mesh=mesh, in_specs=in_specs, out_specs=out_specs, check_vma=False)
```

time: 86.5 us -> 82 us (0.948)
  Pallas kernels: 82.9 us -> 78.4 us
    pallas_call x1, Pallas kernels: 82.9 us -> 78.4 us  [local(): pl.pallas_call(functools.partial(kernel, n_row, child_poles), out_shape=(...]
where the time goes in v2:
time: 82 us; the launch traced here: 81.9 us
  Pallas kernels  78.4 us (96%)
  local copies, waits for them, and re-layouts  2.85 us (3%)
    pallas_call x1, Pallas kernels, local(): pl.pallas_call(functools.partial(kernel, n_row, child_poles), out_shape=(...  78.4 us
    unnamed x4, local copies, waits for them, and re-layouts  2.85 us

profile of v2, /device:TPU:1, one launch (start us, length us, event | category | flops | bytes accessed | tf_op | source)
XLA Modules:
  0.0 81.9 jit_solution(766880256463837720)
XLA Ops:
  0.6 78.4 %shard_map.86 = (f32[2,8,32,512]{3,2,1,0:T(8,128)}, f32[1,512]{1,0:T(1,128)}) custom-call(f32[8,32,256]{2,1,0:T(8,128)} %bitcast.7, f32[8,32,256]{2,1,0:T(8,128)} %bitcast.8, f32[2,256]{1,0:T(2,128)} %poles.1, f32[2,256]{1,0:T(2,128)} %coup.1, s32[2,256]{1,0:T(2,128)} %mask.1, f32[1,512]{1,0:T(1,128)} %bitcast.9, s32[1,512]{1,0:T(1,128)} %bitcast.10), custom_call_target="tpu_custom_call" | custom-call | tf_op jit(solution)/shard_map/pallas_call | solution.py:410
  79.0 0.0 copy-start
  79.0 2.3 %copy.11 = f32[2,256,512]{2,1,0:T(8,128)} copy(f32[2,256,512]{2,1,0:T(8,128)} %bitcast.6) | data formatting | bytes 2097152
  81.3 0.0 copy-done
  81.3 0.6 copy.12
Async XLA Ops:
  79.0 2.3 %copy-start = (f32[1,512]{1,0:T(1,128)S(1)}, f32[1,512]{1,0:T(1,128)}, u32[]{:S(2)}) copy-start(f32[1,512]{1,0:T(1,128)} %get-tuple-element.5) | copy-start | bytes 6148

commit v3 on v2

--- a/solution.py
+++ b/solution.py
@@ -22,12 +22,13 @@
 
 def kernel(
     n_row, child_poles,
-    up, lo, poles, coup, mask, shifts, source,
+    up, lo, poles_in, coup_in, mask_in, shifts_in, source_in,
     out, slab,
-    abuf, ahl, atail, bh, bl, pbuf, rbuf, fbuf, outv,
+    abuf, ahl, atail, bh, bl, pbuf, rbuf, fbuf,
     pwbuf, ssbuf, nsend, nbuf, pcol, wcol, scale, sq, wbuf,
+    poles, coup, mask, shifts, source,
     own_l, own_s, own_r, s1, a1, sf, af, pws, pwr, sss, ssr, ns, nr,
-    rls, rlr, fs, fr, xs, ws, wr, osem,
+    rls, rlr, fs, fr, xs, ws, wr, isem,
 ):
     r = lax.axis_index("row")
     c = lax.axis_index("col")
@@ -40,6 +41,17 @@
     kb = up.shape[2]
     m2 = 2 * half
     nc = shifts.shape[1]
+    fetches = [
+        pltpu.make_async_copy(given, held, isem.at[n])
+        for n, (given, held) in enumerate(
+            zip(
+                (poles_in, coup_in, mask_in, shifts_in, source_in),
+                (poles, coup, mask, shifts, source),
+            )
+        )
+    ]
+    for fetch in fetches:
+        fetch.start()
 
     def at_z(delta, core):
         return (r0 + core, y * NZ + lax.rem(z + delta + NZ, NZ))
@@ -59,6 +71,8 @@
     for dev in peers:
         pl.semaphore_signal(barrier, inc=1, device_id=dev, device_id_type=MESH)
 
+    for fetch in fetches:
+        fetch.wait()
     pw_rows = lax.broadcasted_iota(jnp.int32, (8, kb), 0)
     pole_row = jnp.broadcast_to(poles[pl.ds(k, 1), :], (8, kb))
     weight_row = jnp.broadcast_to(
@@ -249,107 +263,105 @@
         pbuf[3, m, 1] = pbuf[3, m, 1] + rbuf[1, m]
         final(m, 1, 1).start()
 
-    def store(m):
-        return pltpu.make_async_copy(outv.at[:, m], out.at[:, m], osem.at[lax.rem(m, 2)])
-
     def finish(m):
         link(fbuf.at[m], fbuf.at[m], xs.at[0], fr.at[m], other).wait_recv()
         factor = scale[0:1, :]
         mine = (pbuf[0, m, k] + (fbuf[m, 2 * k] + fbuf[m, 2 * k + 1])) * factor
         theirs = (fbuf[m, 4] + (fbuf[m, 2 - 2 * k] + fbuf[m, 3 - 2 * k])) * factor
-        outv[k, m] = mine
-        outv[1 - k, m] = theirs
+        out[k, m] = mine
+        out[1 - k, m] = theirs
         squares = (mine * mine + theirs * theirs).reshape(half // 8, 8, nc)
         sq[...] = sq[...] + jnp.sum(squares, axis=0)
-        @pl.when(m >= 2)
-        def _():
-            store(m - 2).wait()
-
-        store(m).start()
 
     def within(m):
         return jnp.logical_and(m >= 0, m < nm)
 
-    @pl.loop(0, nm + 6)
+    @pl.loop(0, nm + 7)
     def _(t):
+        @pl.when(t < 3)
+        def _():
+            basis_block(3 * t)
+
+        @pl.when(t == 0)
+        def _():
+            all_poles.wait_recv()
+
+        @pl.when(within(t))
+        def _():
+            for d in (0, 1):
+                first_wait(d, t).wait_recv()
+                push(d, t, 0)
+
         @pl.when(within(t - 4))
         def _():
             for d in (0, 1):
                 forward(d, t - 4, 2).wait_recv()
+
             @pl.when(t >= 6)
             def _():
                 sums_sent(t - 6)
+
             multiply_late(t - 4)
 
-        @pl.when(t + LEAD < nm)
-        def _():
-            @pl.when(t + LEAD >= 4)
-            def _():
-                for copy in own_copies(t + LEAD - 4):
-                    copy.wait_send()
-            for copy in own_copies(t + LEAD):
-                copy.start()
-
-        @pl.when(t < 3)
-        def _():
-            basis_block(3 * t)
-
-        @pl.when(t == 0)
-        def _():
-            all_poles.wait_recv()
-
-        @pl.when(within(t))
-        def _():
-            for d in (0, 1):
-                first_wait(d, t).wait_recv()
-                push(d, t, 0)
-
-        @pl.when(t < 3)
-        def _():
-            basis_block(3 * t + 1)
-
-        @pl.when(within(t - 3))
-        def _():
-            split_early(t - 3)
-            multiply_early(t - 3, 2)
-
-        @pl.when(within(t - 1))
-        def _():
-            for d in (0, 1):
-                forward(d, t - 1, 0).wait_recv()
-                push(d, t - 1, 1)
-
-        @pl.when(t < 2)
-        def _():
-            basis_block(3 * t + 2)
-
-        @pl.when(within(t - 3))
-        def _():
-            multiply_early(t - 3, 1)
-
-        @pl.when(within(t - 2))
-        def _():
-            for d in (0, 1):
-                forward(d, t - 2, 1).wait_recv()
-                push(d, t - 2, 2)
-
-        @pl.when(within(t - 3))
-        def _():
-            multiply_early(t - 3, 3)
-            multiply_early(t - 3, 0)
-
-        @pl.when(t == 2)
+        @pl.when(t == 3)
         def _():
             pltpu.make_async_copy(up, abuf.at[0, :, k], own_l).wait()
             link(up, abuf.at[0, :, 1 - k], own_s, own_r, other).wait_recv()
             send_norms()
             nbuf[0] = nsend[0]
 
+        @pl.when(within(t - 3))
+        def _():
+            split_early(t - 3)
+            multiply_early(t - 3, 2)
+
         @pl.when(within(t - 5))
         def _():
             add_relays(t - 5)
 
-        @pl.when(t == 6)
+        @pl.when(t < 3)
+        def _():
+            basis_block(3 * t + 1)
+
+        @pl.when(within(t - 3))
+        def _():
+            multiply_early(t - 3, 1)
+
+        @pl.when(within(t - 3))
+        def _():
+            multiply_early(t - 3, 3)
+
+        @pl.when(within(t - 1))
+        def _():
+            for d in (0, 1):
+                forward(d, t - 1, 0).wait_recv()
+                push(d, t - 1, 1)
+
+        @pl.when(t < 2)
+        def _():
+            basis_block(3 * t + 2)
+
+        @pl.when(within(t - 3))
+        def _():
+            multiply_early(t - 3, 0)
+
+        @pl.when(within(t - 2))
+        def _():
+            for d in (0, 1):
+                forward(d, t - 2, 1).wait_recv()
+                push(d, t - 2, 2)
+
+        @pl.when(t + 3 < nm)
+        def _():
+            @pl.when(t + 3 >= 4)
+            def _():
+                for copy in own_copies(t - 1):
+                    copy.wait_send()
+
+            for copy in own_copies(t + 3):
+                copy.start()
+
+        @pl.when(t == 7)
         def _():
             all_norms.wait_recv()
             total = nbuf[0]
@@ -361,9 +373,9 @@
                 jnp.where(kept, 1.0 / jnp.sqrt(sums), 1.0), (8, nc)
             )
 
-        @pl.when(within(t - 6))
-        def _():
-            finish(t - 6)
+        @pl.when(within(t - 7))
+        def _():
+            finish(t - 7)
 
     wbuf[0] = jnp.sum(sq[...], axis=0, keepdims=True)
     for dlt in range(1, n_row):
@@ -384,7 +396,6 @@
                 forward(d, m, stage).wait_send()
         sums_sent(m)
         added_sent(m)
-        store(m).wait()
 
     weight_sum = wbuf[0]
     all_weights.wait_recv()
@@ -406,15 +417,15 @@
     f32 = jnp.float32
     dma = pltpu.SemaphoreType.DMA
     vmem = pl.BlockSpec(memory_space=pltpu.VMEM)
-    hbm = pl.BlockSpec(memory_space=pl.ANY)
+    hbm = pl.BlockSpec(memory_space=pltpu.HBM)
     out, slab = pl.pallas_call(
         functools.partial(kernel, n_row, child_poles),
         out_shape=(
             jax.ShapeDtypeStruct((2, nm, half, nc), f32),
             jax.ShapeDtypeStruct((1, nc), f32),
         ),
-        in_specs=[hbm, hbm, vmem, vmem, vmem, vmem, vmem],
-        out_specs=(hbm, vmem),
+        in_specs=[hbm] * 7,
+        out_specs=(vmem, vmem),
         scratch_shapes=[
             pltpu.VMEM((NZ, nm, 2, half, kb), f32),
             pltpu.VMEM((2 * m2, kpart - kb), jnp.bfloat16),
@@ -424,7 +435,6 @@
             pltpu.VMEM((NY, nm, 2, half, nc), f32),
             pltpu.VMEM((2, nm, half, nc), f32),
             pltpu.VMEM((nm, 5, half, nc), f32),
-            pltpu.VMEM((2, nm, half, nc), f32),
             pltpu.VMEM((NZ, 8, kb), f32),
             pltpu.VMEM((NY, 2, 8, nc), f32),
             pltpu.VMEM((NY, 8, nc), f32),
@@ -434,25 +444,35 @@
             pltpu.VMEM((8, nc), f32),
             pltpu.VMEM((8, nc), f32),
             pltpu.VMEM((n_row, 1, nc), f32),
+            pltpu.VMEM((2, kb), f32),
+            pltpu.VMEM((2, kb), f32),
+            pltpu.VMEM((2, kb), jnp.int32),
+            pltpu.VMEM((1, nc), f32),
+            pltpu.VMEM((1, nc), jnp.int32),
             dma, dma, dma,
             dma((2, 4, 2)), dma((2, nm)),
             dma((2, 2, 3)), dma((2, nm, 3)),
             dma, dma, dma, dma, dma, dma,
             dma((2, 2)), dma((2, nm)),
             dma((2, 2, 2)), dma((nm,)),
-            dma((2,)), dma, dma, dma((2,)),
+            dma((2,)), dma, dma, dma((5,)),
         ],
         compiler_params=pltpu.CompilerParams(
-            collective_id=0, has_side_effects=True, vmem_limit_bytes=60 * 1024 * 1024
+            collective_id=0, has_side_effects=True, vmem_limit_bytes=50 * 1024 * 1024
         ),
     )(
-        upper_panel.reshape(nm, half, kb),
-        lower_panel.reshape(nm, half, kb),
-        pole_values,
-        coupling,
-        kept_mask,
-        shifts.reshape(1, nc),
-        source.reshape(1, nc),
+        *(
+            pltpu.with_memory_space_constraint(given, pltpu.HBM)
+            for given in (
+                upper_panel.reshape(nm, half, kb),
+                lower_panel.reshape(nm, half, kb),
+                pole_values,
+                coupling,
+                kept_mask,
+                shifts.reshape(1, nc),
+                source.reshape(1, nc),
+            )
+        )
     )
     return out.reshape(2, rows, nc), slab.reshape(nc)
 

time: 82 us -> 78.4 us (0.956)
  Pallas kernels: 78.4 us -> 76.1 us
  local copies, waits for them, and re-layouts: 2.85 us -> 1.55 us
    pallas_call x1, Pallas kernels: 78.4 us -> 76.1 us  [local(): pl.pallas_call(functools.partial(kernel, n_row, child_poles), out_shape=(...]
    unnamed x4 -> x2, local copies, waits for them, and re-layouts: 2.85 us -> 1.55 us
where the time goes in v3:
time: 78.4 us; the launch traced here: 78.3 us
  Pallas kernels  76.1 us (97%)
  local copies, waits for them, and re-layouts  1.55 us (2%)
    pallas_call x1, Pallas kernels, local(): pl.pallas_call(functools.partial(kernel, n_row, child_poles), out_shape=(...  76.1 us

profile of v3, /device:TPU:1, one launch (start us, length us, event | category | flops | bytes accessed | tf_op | source)
XLA Modules:
  0.0 78.3 jit_solution(16386173366702551743)
XLA Ops:
  0.6 76.1 %shard_map.86 = (f32[2,8,32,512]{3,2,1,0:T(8,128)S(1)}, f32[1,512]{1,0:T(1,128)S(1)}) custom-call(f32[8,32,256]{2,1,0:T(8,128)} %bitcast.8, f32[8,32,256]{2,1,0:T(8,128)} %bitcast.9, f32[2,256]{1,0:T(2,128)} %poles_in.1, f32[2,256]{1,0:T(2,128)} %coup_in.1, s32[2,256]{1,0:T(2,128)} %mask_in.1, f32[1,512]{1,0:T(1,128)} %bitcast.10, s32[1,512]{1,0:T(1,128)} %bitcast.11), custom_call_target="tpu_custom_call" | custom-call | tf_op jit(solution)/shard_map/pallas_call | solution.py:421
  76.8 1.0 %copy.11 = f32[2,256,512]{2,1,0:T(8,128)} copy(f32[2,256,512]{2,1,0:T(8,128)S(1)} %bitcast.6) | data formatting | bytes 2097152
  77.7 0.6 copy.12

commit v4 on v3

--- a/solution.py
+++ b/solution.py
@@ -150,6 +150,11 @@
         wcol[...] = jnp.broadcast_to(pw[1:2, :], (128, kb)).T
         first = k * child_poles + (y * NZ + lax.rem(z + rel, NZ)) * kb
 
+        tall = (block_rows // 8, 8, 128)
+        ids = (
+            lax.broadcasted_iota(jnp.int32, tall, 0) * 8 + lax.broadcasted_iota(jnp.int32, tall, 1)
+        ).astype(jnp.float32)
+
         @pl.loop(0, NY * (nc // 128))
         def _(tile):
             dest = lax.div(tile, nc // 128)
@@ -165,12 +170,8 @@
                 weight = wcol[rows, :].reshape(shape)
                 cauchy = weight / (pole - shift[None])
                 total = total + jnp.sum(cauchy * cauchy, axis=0)
-                ids = (
-                    lax.broadcasted_iota(jnp.int32, shape, 0) * 8
-                    + lax.broadcasted_iota(jnp.int32, shape, 1)
-                    + (first + rb * block_rows)
-                ).astype(jnp.float32)
-                hot = jnp.where(ids == named[None], 1.0, 0.0)
+                at_row_here = named - (first + rb * block_rows).astype(jnp.float32)
+                hot = jnp.where(ids == at_row_here[None], 1.0, 0.0)
                 value = jnp.where(kept[None], cauchy, hot).reshape(block_rows, 128)
                 high = value.astype(jnp.bfloat16)
                 low = (value - high.astype(jnp.float32)).astype(jnp.bfloat16)

time: 78.4 us -> 78.3 us (level)
  no operation moved by 1% of the time
where the time goes in v4:
time: 78.3 us; the launch traced here: 78.2 us
  Pallas kernels  76 us (97%)
  local copies, waits for them, and re-layouts  1.55 us (2%)
    pallas_call x1, Pallas kernels, local(): pl.pallas_call(functools.partial(kernel, n_row, child_poles), out_shape=(...  76 us

profile of v4, /device:TPU:1, one launch (start us, length us, event | category | flops | bytes accessed | tf_op | source)
XLA Modules:
  0.0 78.2 jit_solution(15380963095239025169)
XLA Ops:
  0.6 76.0 %shard_map.86 = (f32[2,8,32,512]{3,2,1,0:T(8,128)S(1)}, f32[1,512]{1,0:T(1,128)S(1)}) custom-call(f32[8,32,256]{2,1,0:T(8,128)} %bitcast.8, f32[8,32,256]{2,1,0:T(8,128)} %bitcast.9, f32[2,256]{1,0:T(2,128)} %poles_in.1, f32[2,256]{1,0:T(2,128)} %coup_in.1, s32[2,256]{1,0:T(2,128)} %mask_in.1, f32[1,512]{1,0:T(1,128)} %bitcast.10, s32[1,512]{1,0:T(1,128)} %bitcast.11), custom_call_target="tpu_custom_call" | custom-call | tf_op jit(solution)/shard_map/pallas_call | solution.py:422
  76.6 1.0 %copy.11 = f32[2,256,512]{2,1,0:T(8,128)} copy(f32[2,256,512]{2,1,0:T(8,128)S(1)} %bitcast.6) | data formatting | bytes 2097152
  77.6 0.6 copy.12

commit v5 on v4

--- a/solution.py
+++ b/solution.py
@@ -10,7 +10,7 @@
 NZ = 8
 NY = 4
 CHUNKS = 8
-LEAD = 3
+LEAD = 4
 MESH = pl.DeviceIdType.MESH
 
 
@@ -352,14 +352,14 @@
                 forward(d, t - 2, 1).wait_recv()
                 push(d, t - 2, 2)
 
-        @pl.when(t + 3 < nm)
-        def _():
-            @pl.when(t + 3 >= 4)
+        @pl.when(t + 4 < nm)
+        def _():
+            @pl.when(t + 4 >= 4)
             def _():
-                for copy in own_copies(t - 1):
+                for copy in own_copies(t):
                     copy.wait_send()
 
-            for copy in own_copies(t + 3):
+            for copy in own_copies(t + 4):
                 copy.start()
 
         @pl.when(t == 7)

time: 78.3 us -> 77.5 us (0.990)
  Pallas kernels: 76 us -> 75.2 us
    pallas_call x1, Pallas kernels: 76 us -> 75.2 us  [local(): pl.pallas_call(functools.partial(kernel, n_row, child_poles), out_shape=(...]
where the time goes in v5:
time: 77.5 us; the launch traced here: 77.3 us
  Pallas kernels  75.2 us (97%)
  local copies, waits for them, and re-layouts  1.55 us (2%)
    pallas_call x1, Pallas kernels, local(): pl.pallas_call(functools.partial(kernel, n_row, child_poles), out_shape=(...  75.2 us
    unnamed x2, local copies, waits for them, and re-layouts  1.55 us

profile of v5, /device:TPU:1, one launch (start us, length us, event | category | flops | bytes accessed | tf_op | source)
XLA Modules:
  0.0 77.3 jit_solution(4368618347830837805)
XLA Ops:
  0.6 75.2 %shard_map.86 = (f32[2,8,32,512]{3,2,1,0:T(8,128)S(1)}, f32[1,512]{1,0:T(1,128)S(1)}) custom-call(f32[8,32,256]{2,1,0:T(8,128)} %bitcast.8, f32[8,32,256]{2,1,0:T(8,128)} %bitcast.9, f32[2,256]{1,0:T(2,128)} %poles_in.1, f32[2,256]{1,0:T(2,128)} %coup_in.1, s32[2,256]{1,0:T(2,128)} %mask_in.1, f32[1,512]{1,0:T(1,128)} %bitcast.10, s32[1,512]{1,0:T(1,128)} %bitcast.11), custom_call_target="tpu_custom_call" | custom-call | tf_op jit(solution)/shard_map/pallas_call | solution.py:422
  75.8 1.0 %copy.11 = f32[2,256,512]{2,1,0:T(8,128)} copy(f32[2,256,512]{2,1,0:T(8,128)S(1)} %bitcast.6) | data formatting | bytes 2097152
  76.8 0.6 copy.12

commit v6 on v5

--- a/solution.py
+++ b/solution.py
@@ -10,7 +10,7 @@
 NZ = 8
 NY = 4
 CHUNKS = 8
-LEAD = 4
+LEAD = 5
 MESH = pl.DeviceIdType.MESH
 
 
@@ -92,7 +92,7 @@
         return [
             link(
                 panels[child].at[m], abuf.at[NZ - 1 if step == 1 else 1, m, k],
-                s1.at[d, lax.rem(m, 4), child], a1.at[d, m], at_z(step, child),
+                s1.at[d, m, child], a1.at[d, m], at_z(step, child),
             )
             for d, step in ((0, 1), (1, NZ - 1))
             for child in (0, 1)
@@ -352,14 +352,9 @@
                 forward(d, t - 2, 1).wait_recv()
                 push(d, t - 2, 2)
 
-        @pl.when(t + 4 < nm)
-        def _():
-            @pl.when(t + 4 >= 4)
-            def _():
-                for copy in own_copies(t):
-                    copy.wait_send()
-
-            for copy in own_copies(t + 4):
+        @pl.when(t + 5 < nm)
+        def _():
+            for copy in own_copies(t + 5):
                 copy.start()
 
         @pl.when(t == 7)
@@ -388,7 +383,7 @@
     link(up, abuf.at[0, :, k], own_s, own_r, other).wait_send()
     all_norms.wait_send()
 
-    for m in range(nm - 4, nm):
+    for m in range(nm):
         for copy in own_copies(m):
             copy.wait_send()
     for m in range(nm - 2, nm):
@@ -451,7 +446,7 @@
             pltpu.VMEM((1, nc), f32),
             pltpu.VMEM((1, nc), jnp.int32),
             dma, dma, dma,
-            dma((2, 4, 2)), dma((2, nm)),
+            dma((2, nm, 2)), dma((2, nm)),
             dma((2, 2, 3)), dma((2, nm, 3)),
             dma, dma, dma, dma, dma, dma,
             dma((2, 2)), dma((2, nm)),

time: 77.5 us -> 78 us (level)
  no operation moved by 1% of the time
where the time goes in v6:
time: 78 us; the launch traced here: 77.9 us
  Pallas kernels  75.7 us (97%)
  local copies, waits for them, and re-layouts  1.55 us (2%)
    pallas_call x1, Pallas kernels, local(): pl.pallas_call(functools.partial(kernel, n_row, child_poles), out_shape=(...  75.7 us

profile of v6, /device:TPU:1, one launch (start us, length us, event | category | flops | bytes accessed | tf_op | source)
XLA Modules:
  0.0 77.9 jit_solution(2902155512986631414)
XLA Ops:
  0.6 75.7 %shard_map.86 = (f32[2,8,32,512]{3,2,1,0:T(8,128)S(1)}, f32[1,512]{1,0:T(1,128)S(1)}) custom-call(f32[8,32,256]{2,1,0:T(8,128)} %bitcast.8, f32[8,32,256]{2,1,0:T(8,128)} %bitcast.9, f32[2,256]{1,0:T(2,128)} %poles_in.1, f32[2,256]{1,0:T(2,128)} %coup_in.1, s32[2,256]{1,0:T(2,128)} %mask_in.1, f32[1,512]{1,0:T(1,128)} %bitcast.10, s32[1,512]{1,0:T(1,128)} %bitcast.11), custom_call_target="tpu_custom_call" | custom-call | tf_op jit(solution)/shard_map/pallas_call | solution.py:417
  76.4 1.0 %copy.11 = f32[2,256,512]{2,1,0:T(8,128)} copy(f32[2,256,512]{2,1,0:T(8,128)S(1)} %bitcast.6) | data formatting | bytes 2097152
  77.4 0.6 copy.12
